TPU v7x, 32 devices: a whole 2x2x4 slice. The times are simulated.
32 devices in a mesh: tm: 16 (over z, y, x), mp: 2 (over core).
Axes of the slice: x: 2, y: 2, z: 4, core: 2. Of those that a mesh axis runs over, the one named last changes fastest.
Arguments:
- frames: bfloat16 [5120, 1024], P('tm'), may hold values from -6 to 6
- valid: int32 [5120], P('tm'), may hold values from 0 to 1, as said below
- norm_gain: float32 [1024], replicated, may hold values from 0.1 to 1.9
- norm_bias: float32 [1024], replicated, may hold values from -3 to 3
- w_qkv: bfloat16 [3, 1024, 1024], P(None, None, 'mp'), may hold values from -8 to 8
- w_out: bfloat16 [1024, 1024], P(None, 'mp'), may hold values from -0.1875 to 0.1875
- conv_weight: float32 [9, 1024], P(None, 'mp'), may hold values from -2 to 2
- conv_scale: float32 [1024], P('mp'), may hold values from 0.5 to 2
- conv_shift: float32 [1024], P('mp'), may hold values from -3 to 3
Outputs:
- encoded: bfloat16 [5120, 1024], P('tm', 'mp')
Inputs may be any that keep to these rules, and one draw needn't show every extreme that they name: valid is 1 on a prefix of the frames and 0 on a final run of 1 to 128 frames.
All inputs are finite; a program needn't handle non-finite values.
Results may differ from a plain program's by a relative error of at most 0.0059.
Values may be sent and summed in bfloat16 or wider, within the bound.
No kernel may reach another device: no remote copies, remote signals or barrier semaphores. Data moves between devices by JAX's collectives and lax.ppermute only.
A program may use at most 64 MiB of HBM per device.

v0:
```python
import math

import jax
import jax.numpy as jnp
from jax import lax
from jax.experimental import pallas as pl
from jax.experimental.pallas import tpu as pltpu
from jax.sharding import PartitionSpec as P

HEAD_DIM = 128
CTX = 128
KERNEL = 9
EXT = 8
HALO = CTX + EXT
FAR = KERNEL // 2
LANES = 128
MIDDLE = KERNEL // 2
MOVED = [tap for tap in range(KERNEL) if tap != MIDDLE]
PAD = 16
SPAN = CTX + PAD + CTX
NEG = -1e30
GROUP = 2
WARM_FLOPS, PICK_FLOPS, NORM_FLOPS = 1_500_000_000, 1_000_000_000, 1_500_000_000
SCALE = math.log2(math.e) / math.sqrt(HEAD_DIM)
VMEM = pl.BlockSpec(memory_space=pltpu.VMEM)
ANY = pl.BlockSpec(memory_space=pl.ANY)
SMEM = pl.BlockSpec(memory_space=pltpu.SMEM)
F32, BF16 = jnp.float32, jnp.bfloat16


def layer_normed(values, gain, bias):
    center = values - jnp.mean(values, axis=-1, keepdims=True)
    spread = jnp.mean(center * center, axis=-1, keepdims=True)
    return center * lax.rsqrt(spread + 1e-05) * gain + bias


def norm_rows(source, source_at, target, target_at, count, gain, bias):
    step = 16
    for at in range(0, count, step):
        size = min(step, count - at)
        values = source[rows_at(source_at + at, size), :].astype(F32)
        target[target_at + at : target_at + at + size, :] = layer_normed(
            values, gain, bias
        ).astype(BF16)


def dot(a, b):
    return jnp.dot(a, b, preferred_element_type=F32)


def dot_t(a, b):
    return lax.dot_general(a, b, (((1,), (1,)), ((), ())), preferred_element_type=F32)


def positions(shape, dim, start):
    return lax.broadcasted_iota(jnp.int32, shape, dim) + start


def rows_at(start, size):
    return pl.ds(pl.multiple_of(start, 8), size)


def lane_blocks(width):
    return [slice(at, at + LANES) for at in range(0, width, LANES)]


def pick_kernel(frames, after, sent):
    p = lax.axis_index("mp")
    rows, width = frames.shape
    blocks = lane_blocks(width)
    near = rows_at((1 - p) * (rows - CTX), CTX)
    for i, lanes in enumerate(blocks):
        sent[i * CTX : (i + 1) * CTX, :] = frames[near, lanes]
    far = frames[rows_at((1 - p) * (rows - HALO) + p * CTX, EXT), :].astype(F32)
    far = jnp.where(p == 0, pltpu.roll(far, EXT - FAR, 0), far)
    sent[len(blocks) * CTX :, :] = jnp.concatenate(
        [far[:FAR, lanes] for lanes in blocks], axis=0
    ).astype(BF16)


def halo_rows(halo, start, size, blocks):
    return jnp.concatenate(
        [halo[rows_at(i * CTX + start, size), :].astype(F32) for i in blocks], axis=1
    )


def own_heads(normed, w, count, q_out, k_out, v_out, top_out, total_out, acc_out, att_out):
    p = lax.axis_index("mp")
    keys, queries = k_out.shape[0], q_out.shape[0]
    rows = 2 * (queries - EXT)
    key_at, query_at = p * (rows - keys), p * (rows - queries)
    k_out[...] = dot(normed[...], w[1]).astype(BF16)
    picked = normed[pl.ds(pl.multiple_of(p * (keys - queries), 16), queries), :]
    q_out[...] = (dot(picked, w[0]) * SCALE).astype(BF16)
    v_out[...] = dot(normed[...], w[2]).astype(BF16)
    key_pos = positions((queries, keys), 1, key_at)
    query_pos = positions((queries, keys), 0, query_at)
    allowed = (jnp.abs(key_pos - query_pos) <= CTX) & (key_pos < count)
    for head in range(q_out.shape[1] // HEAD_DIM):
        at = slice(head * HEAD_DIM, (head + 1) * HEAD_DIM)
        scores = dot_t(q_out[:, at], k_out[:, at])
        scores = jnp.where(allowed, scores, NEG)
        top = jnp.max(scores, axis=-1, keepdims=True)
        raised = jnp.exp2(scores - top)
        total = jnp.sum(raised, axis=-1, keepdims=True)
        top_out[head] = jnp.broadcast_to(top, (queries, HEAD_DIM))
        total_out[head] = jnp.broadcast_to(total, (queries, HEAD_DIM))
        acc = dot(raised.astype(BF16), v_out[:, at])
        acc_out[:, at] = acc
        att_out[:, at] = (acc * (1.0 / total)).astype(BF16)


def norm_kernel(frames, valid, gain, bias, normed, count_here):
    p = lax.axis_index("mp")
    rows, keys = frames.shape[0], normed.shape[0]
    low, high = jnp.int32(0), jnp.int32(rows)
    for _ in range(rows.bit_length()):
        middle = (low + high) // 2
        one = valid[jnp.minimum(middle, rows - 1)] > 0
        open_ = low < high
        low = jnp.where(open_ & one, middle + 1, low)
        high = jnp.where(open_ & jnp.logical_not(one), middle, high)
    count_here[...] = jnp.full(count_here.shape, low, jnp.int32)
    norm_rows(frames, p * (rows - keys), normed, 0, keys, gain[...], bias[...])


def first_kernel(normed, w, count_here, q, k, v, top, total, acc, att):
    keys = k.shape[0]
    count = jnp.concatenate([count_here[0:1, :]] * pl.cdiv(keys, count_here.shape[1]), axis=1)[:, :keys]
    own_heads(normed, w, count, q, k, v, top, total, acc, att)


def block_time(index, core, queries, rows):
    edge = jnp.where(core == 0, -EXT, rows)
    return jnp.where(index < queries, index + core * (rows - queries), index - queries + edge)


def block_mask(index, core, queries, rows, count):
    tm, last = lax.axis_index("tm"), lax.axis_size("tm") - 1
    time = block_time(index, core, queries, rows)
    low = jnp.where(tm > 0, -EXT, 0)
    high = jnp.where(tm < last, rows + EXT, count)
    return jnp.where((time >= low) & (time < high), 1.0, 0.0)


def warm_kernel(own_shift, other_shift):
    p = lax.axis_index("mp")
    for out, core in ((own_shift, p), (other_shift, 1 - p)):
        half, width = out.shape[0] // len(MOVED), out.shape[1]
        time = block_time(positions((1, width), 1, 0), core, width - EXT, 2 * half)
        for i, tap in enumerate(MOVED):
            row = positions((half, width), 0, core * half + tap - KERNEL // 2)
            out[i * half : (i + 1) * half, :] = jnp.where(row == time, 1.0, 0.0).astype(BF16)


def mask_shift(shift, core, count, out, mask_out):
    half, width = out.shape[0] // len(MOVED), out.shape[1]
    queries, rows = width - EXT, 2 * half
    mask = block_mask(positions((1, width), 1, 0), core, queries, rows, count[0:1, :width])
    mask = mask.astype(BF16)
    for i in range(len(MOVED)):
        at = slice(i * half, (i + 1) * half)
        out[at, :] = shift[at, :] * mask
    index = positions(mask_out.shape, 0, 0)
    mask_out[...] = block_mask(index, core, queries, rows, count[0:1, : mask_out.shape[1]])


def second_kernel(
    normed,
    w,
    count_here,
    own_base,
    other_base,
    q,
    k,
    v,
    top,
    total,
    acc,
    att,
    own_shift,
    other_shift,
    own_mask,
    other_mask,
):
    p = lax.axis_index("mp")
    first_kernel(normed, w, count_here, q, k, v, top, total, acc, att)
    mask_shift(own_base, p, count_here, own_shift, own_mask)
    mask_shift(other_base, 1 - p, count_here, other_shift, other_mask)


def halo_kernel(halo, frames, gain, bias, wo, *refs):
    parts = (refs[:8], refs[8:16])
    send, att_all, normed, kx, vx = refs[16:]
    p = lax.axis_index("mp")
    last = lax.axis_size("tm") - 1
    tm = lax.axis_index("tm")
    rows, queries, keys = frames.shape[0], refs[1].shape[0], refs[2].shape[0]
    width = refs[1].shape[1]
    heads = width // HEAD_DIM
    present = jnp.where(p == 0, tm > 0, tm < last)
    norms = (gain[...], bias[...])
    blocks = range(frames.shape[1] // LANES)
    ext = halo_rows(halo, (CTX - EXT) * (1 - p), EXT, blocks)
    row = positions(ext.shape, 0, 0)
    fixed = jnp.where(row == 0, gain[...], jnp.where(row == 1, bias[...], 0.0))
    left = jnp.concatenate([ext * gain[...], fixed], axis=0)
    high = left.astype(BF16)
    left = left - high.astype(F32)
    middle = left.astype(BF16)
    low = (left - middle.astype(F32)).astype(BF16)
    left = jnp.concatenate([high, middle, low], axis=0)
    ext_mean = jnp.mean(ext, axis=-1, keepdims=True)
    ext_center = ext - ext_mean
    ext_scale = lax.rsqrt(jnp.mean(ext_center * ext_center, axis=-1, keepdims=True) + 1e-05)
    q_ext = []
    for w, *_ in parts:
        thirds = dot(left, w[0])
        whole = thirds[: 2 * EXT] + thirds[2 * EXT : 4 * EXT] + thirds[4 * EXT :]
        q = (whole[:EXT] - ext_mean * whole[EXT : EXT + 1]) * ext_scale
        q_ext.append((q + whole[EXT + 1 : EXT + 2]) * SCALE)
    q_ext = jnp.concatenate(q_ext, axis=1)
    near = halo_rows(halo, 0, CTX, blocks)
    normed[:CTX, :] = layer_normed(near, *norms).astype(BF16)
    far = halo[len(blocks) * CTX :, :].astype(F32)
    far = jnp.concatenate([far[i * FAR : (i + 1) * FAR] for i in blocks], axis=1)
    far = jnp.concatenate([far, jnp.zeros((EXT - FAR, far.shape[1]), F32)], axis=0)
    normed[CTX:, :] = layer_normed(far, *norms).astype(BF16)
    near_at = jnp.where(p == 0, -CTX, rows)
    far_at = jnp.where(p == 0, -(CTX + FAR), rows + CTX)
    ext_at = jnp.where(p == 0, -EXT, rows)
    part = rows_at(p * (queries - CTX), CTX)
    rest = rows_at((1 - p) * CTX, queries - CTX)
    own = rows_at(p * (keys - CTX), CTX)
    own_pos = p * (rows - CTX)
    blank = jnp.zeros((PAD - EXT, width), F32)
    query_pos = positions((CTX, CTX), 0, p * (rows - CTX))
    near_pos = positions((CTX, CTX), 1, near_at)
    allowed = (jnp.abs(near_pos - query_pos) <= CTX) & present
    each = [
        (side, head, slice(head * HEAD_DIM, (head + 1) * HEAD_DIM))
        for side in range(2)
        for head in range(heads)
    ]

    def lanes_of(side, at):
        return slice(side * width + at.start, side * width + at.stop)

    for side, (w, q, k, v, top_own, total_own, acc_own, att) in enumerate(parts):
        to = slice(side * width, (side + 1) * width)
        kx[CTX + PAD :, to] = k[own, :]
        vx[CTX + PAD :, to] = v[own, :]
        att_all[CTX + PAD : CTX + PAD + queries - CTX, to] = att[rest, :]

    def project(x, i, sides):
        for side in sides:
            w = parts[side][0]
            to = slice(side * width, (side + 1) * width)
            got = dot(normed[...], w[i])
            x[:CTX, to] = got[:CTX].astype(BF16)
            x[CTX : CTX + PAD, to] = jnp.concatenate([got[CTX:], blank], axis=0).astype(BF16)

    scores = []
    project(kx, 1, (0, 1))
    deep = 2 * heads * EXT
    tiled = jnp.concatenate([q_ext] * (2 * heads), axis=0)
    head_of_row = positions(tiled.shape, 0, 0) // EXT
    head_of_lane = positions(tiled.shape, 1, 0) // HEAD_DIM
    tiled = jnp.where(head_of_row == head_of_lane, tiled, 0.0).astype(BF16)
    project(vx, 2, (0,))
    scores += [
        dot_t(parts[i][1][part, at], kx[:CTX, lanes_of(i, at)]) for i, head, at in each if i == 0
    ]
    scores += [
        dot_t(parts[i][1][part, at], kx[:CTX, lanes_of(i, at)]) for i, head, at in each if i == 1
    ]
    ext_scores = dot_t(tiled, kx[...])
    project(vx, 2, (1,))
    raised, total, faded = [], [], []
    for (side, head, at), score in zip(each, scores):
        top_own, total_own = parts[side][4], parts[side][5]
        score = jnp.where(allowed, score, NEG)
        before = top_own[head, part, :]
        top = jnp.maximum(before, jnp.max(score, axis=-1, keepdims=True))
        up = jnp.exp2(score - top)
        faded.append(jnp.exp2(before - top))
        total.append(
            total_own[head, part, :] * faded[-1] + jnp.sum(up, axis=-1, keepdims=True)
        )
        raised.append(up.astype(BF16))
    column = positions((deep, SPAN), 1, 0)
    key_pos = jnp.where(
        column < CTX,
        column + near_at,
        jnp.where(column < CTX + FAR, column - CTX + far_at, column - (CTX + PAD) + own_pos),
    )
    row_pos = positions((deep, SPAN), 0, 0) % EXT + ext_at
    seen = (jnp.abs(key_pos - row_pos) <= CTX) & ((column < CTX + FAR) | (column >= CTX + PAD))
    ext_scores = jnp.where(seen, ext_scores, NEG)
    ext_up = jnp.exp2(ext_scores - jnp.max(ext_scores, axis=-1, keepdims=True))
    ext_total = jnp.sum(ext_up, axis=-1, keepdims=True)
    gathered = [
        dot(up, vx[:CTX, lanes_of(side, at)]) for (side, head, at), up in zip(each, raised)
    ]
    spread = dot(ext_up.astype(BF16), vx[...]) * (1.0 / ext_total)
    for i, (side, head, at) in enumerate(each):
        acc = parts[side][6][part, at] * faded[i] + gathered[i]
        att_all[:CTX, lanes_of(side, at)] = (acc / total[i]).astype(BF16)
    ext_att = jnp.concatenate(
        [
            spread[h * EXT : (h + 1) * EXT, h * HEAD_DIM : (h + 1) * HEAD_DIM]
            for h in range(2 * heads)
        ],
        axis=1,
    )
    att_all[CTX : CTX + PAD, :] = jnp.concatenate(
        [ext_att, jnp.zeros_like(ext_att)], axis=0
    ).astype(BF16)
    mix(att_all, frames, halo, wo, 1 - p, send)


def mix(att_all, frames, halo, wo, columns, out):
    p = lax.axis_index("mp")
    rows, width = frames.shape[0], out.shape[1]
    queries = out.shape[0] - EXT
    other = queries - CTX
    lanes = pl.ds(pl.multiple_of(columns * width, width), width)
    projected = 0.0
    for side in range(2):
        for at in range(0, width, 2 * HEAD_DIM):
            first = (p if side == 0 else 1 - p) * width + at
            pair = wo[pl.ds(pl.multiple_of(first, 128), 2 * HEAD_DIM), :]
            at += side * width
            projected = projected + dot(att_all[:, at : at + 2 * HEAD_DIM], pair)

    def put(plain, to, size, at):
        out[rows_at(to, size), :] = (plain + projected[at : at + size]).astype(BF16)

    def own(at, size):
        return frames[rows_at(p * (rows - queries) + at, size), lanes].astype(F32)

    put(own(p * other, CTX), p * other, CTX, 0)
    count = width // LANES
    blocks = [columns * count + i for i in range(count)]
    put(halo_rows(halo, (CTX - EXT) * (1 - p), EXT, blocks), queries, EXT, CTX)
    put(own((1 - p) * CTX, other), (1 - p) * CTX, other, CTX + PAD)


def keep_kernel(att_all, frames, halo, wo, keep):
    mix(att_all, frames, halo, wo, lax.axis_index("mp"), keep)


def convolved(block, core, shift_by, mask, weight, scale, shift, store):
    half = shift_by.shape[0] // len(MOVED)
    rows = rows_at(core * (block.shape[0] - EXT - half), half)
    step = 2 * LANES
    valid = jnp.concatenate([mask[rows, :]] * (step // mask.shape[1]), axis=1)
    for at in range(0, block.shape[1], step):
        lanes = slice(at, at + step)
        gain = 0.5 * scale[:, lanes]
        plain = block[rows, lanes].astype(F32)
        u = plain * valid * (weight[MIDDLE : MIDDLE + 1, lanes] * gain) + 0.5 * shift[:, lanes]
        for first in range(0, len(MOVED), GROUP):
            group = MOVED[first : first + GROUP]
            moved = dot(shift_by[first * half : (first + len(group)) * half, :], block[:, lanes])
            for i, tap in enumerate(group):
                part = moved[i * half : (i + 1) * half]
                u = u + part * (weight[tap : tap + 1, lanes] * gain)
        store(lanes, (plain + (u + u * jnp.tanh(u))).astype(BF16))


def own_conv_kernel(keep, shift_by, mask, weight, scale, shift, out):
    def store(lanes, value):
        out[:, lanes] = value

    core = lax.axis_index("mp")
    convolved(keep, core, shift_by, mask, weight, scale, shift, store)


def other_conv_kernel(got, done, shift_by, mask, weight, scale, shift, out, block, sems):
    core = 1 - lax.axis_index("mp")
    half = done.shape[0]
    first = pltpu.make_async_copy(done, out.at[rows_at((1 - core) * half, half), :], sems.at[0])
    first.start()
    copies = [first]

    def store(lanes, value):
        block[:, lanes] = value
        copies.append(
            pltpu.make_async_copy(
                block.at[:, lanes], out.at[rows_at(core * half, half), lanes], sems.at[len(copies)]
            )
        )
        copies[-1].start()

    convolved(got, core, shift_by, mask, weight, scale, shift, store)
    for copy in copies:
        copy.wait()


def call(kernel, out_shape, in_specs, out_specs, scratch=(), flops=0, size=0, exps=0, limit=16):
    return pl.pallas_call(
        kernel,
        out_shape=out_shape,
        in_specs=in_specs,
        out_specs=out_specs,
        scratch_shapes=scratch,
        compiler_params=pltpu.CompilerParams(vmem_limit_bytes=limit << 20),
        cost_estimate=pl.CostEstimate(flops=flops, bytes_accessed=size, transcendentals=exps),
    )


def compute(frames, valid, norm_gain, norm_bias, w_qkv, w_out, conv_weight, conv_scale, conv_shift):
    rows, model = frames.shape
    width = w_qkv.shape[2]
    heads = width // HEAD_DIM
    count = lax.axis_size("tm")
    half = rows // 2
    queries = half + EXT
    keys = half + EXT + CTX
    block = queries + EXT
    assert rows >= HALO + CTX and rows % 32 == 0
    shaped = jax.ShapeDtypeStruct
    pairs = [(1, 0), (2 * count - 2, 2 * count - 1)]
    for i in range(count - 1):
        pairs += [(2 * i, 2 * (i + 1)), (2 * (i + 1) + 1, 2 * i + 1)]
    other = [(0, 1), (1, 0)]
    shift_shapes = (shaped((len(MOVED) * half, block), BF16),) * 2
    shifts = call(warm_kernel, shift_shapes, [], (VMEM,) * 2, flops=WARM_FLOPS)()
    sent = call(
        pick_kernel,
        shaped(((CTX + FAR) * (model // LANES), LANES), BF16),
        [VMEM, ANY],
        VMEM,
        flops=PICK_FLOPS,
    )(frames, shifts[0])
    halo = lax.ppermute(sent, ("tm", "mp"), pairs)
    w_other = lax.ppermute(w_qkv, "mp", other)
    wo_other = lax.ppermute(w_out, "mp", other)
    gain, bias = norm_gain.reshape(1, model), norm_bias.reshape(1, model)
    results = (
        shaped((queries, width), BF16),
        shaped((keys, width), BF16),
        shaped((keys, width), BF16),
        shaped((heads, queries, HEAD_DIM), F32),
        shaped((heads, queries, HEAD_DIM), F32),
        shaped((queries, width), F32),
        shaped((queries, width), BF16),
    )
    normed, count_here = call(
        norm_kernel,
        (shaped((keys, model), BF16), shaped((8, 256), jnp.int32)),
        [VMEM, SMEM, VMEM, VMEM],
        (VMEM,) * 2,
        flops=NORM_FLOPS,
        size=1_000_000,
    )(frames, valid, gain, bias)
    mine = call(
        first_kernel,
        results,
        [VMEM] * 3,
        (VMEM,) * 7,
        flops=1_300_000_000,
        size=4_000_000,
        exps=300_000,
    )(normed, w_qkv, count_here)
    second = call(
        second_kernel,
        results + shift_shapes + (shaped((block, LANES), F32),) * 2,
        [VMEM] * 5,
        (VMEM,) * 11,
        flops=1_300_000_000,
        size=4_000_000,
        exps=300_000,
    )(normed, w_other, count_here, *shifts)
    theirs, (own_shift, other_shift, own_mask, other_mask) = second[:7], second[7:]
    send, att_all = call(
        halo_kernel,
        (shaped((block, width), BF16), shaped((pl.cdiv(queries, 16) * 16 + PAD, model), BF16)),
        [VMEM] * 21,
        (VMEM,) * 2,
        [
            pltpu.VMEM((HALO, model), BF16),
            pltpu.VMEM((SPAN, model), BF16),
            pltpu.VMEM((SPAN, model), BF16),
        ],
        flops=1_500_000_000,
        size=10_000_000,
        exps=300_000,
    )(halo, frames, gain, bias, wo_other, w_qkv, *mine, w_other, *theirs)
    got = lax.ppermute(send, "mp", other)
    keep = call(
        keep_kernel,
        shaped((block, width), BF16),
        [VMEM] * 4,
        VMEM,
        flops=200_000_000,
        size=1_000_000,
    )(att_all, frames, halo, w_out)
    weights = (conv_weight, conv_scale.reshape(1, width), conv_shift.reshape(1, width))
    done = call(
        own_conv_kernel,
        shaped((half, width), BF16),
        [VMEM] * 6,
        VMEM,
        flops=270_000_000,
        size=1_000_000,
    )(keep, own_shift, own_mask, *weights)
    return call(
        other_conv_kernel,
        shaped((rows, width), BF16),
        [VMEM] * 7,
        ANY,
        [pltpu.VMEM((half, width), BF16), pltpu.SemaphoreType.DMA((1 + width // 256,))],
        flops=270_000_000,
        size=1_000_000,
    )(got, done, other_shift, other_mask, *weights)


def solution(mesh):
    placed = (
        P("tm", None),
        P("tm"),
        P(),
        P(),
        P(None, None, "mp"),
        P(None, "mp"),
        P(None, "mp"),
        P("mp"),
        P("mp"),
    )
    return jax.shard_map(
        compute, mesh=mesh, in_specs=placed, out_specs=P("tm", "mp"), check_vma=False
    )
```

profile of v0, /device:TPU:0, one launch (start us, length us, event | category | flops | bytes accessed | tf_op | source)
XLA Modules:
  0.0 15.8 jit_solution(2670607847906752992)
XLA Ops:
  0.0 0.0 copy-start.1
  0.0 0.5 %collective-permute-start.2 = (bf16[3,1024,512]{2,1,0:T(8,128)(2,1)}, bf16[3,1024,512]{2,1,0:T(8,128)(2,1)S(1)}, u32[]{:S(2)}, u32[]{:S(2)}) collective-permute-start(bf16[3,1024,512]{2,1,0:T(8,128)(2,1)} %refs_0_.1), channel_id=1, source_target_pairs={{0,1},{1,0},{2,3},{3,2},{4,5},{5,4},{6,7},{7,6},{8,9},{9,8},{10,11... | collective-permute-start | bytes 9437192 | tf_op jit(solution)/shard_map/ppermute | solution.py:438
  0.5 0.1 collective-permute-start.1
  0.6 0.3 %shard_map.91 = (bf16[1280,176]{1,0:T(8,128)(2,1)S(1)}, bf16[1280,176]{1,0:T(8,128)(2,1)S(1)}) custom-call(), custom_call_target="tpu_custom_call" | custom-call | flops 1500000000 | tf_op jit(solution)/shard_map/pallas_call | solution.py:429
  0.8 0.0 copy-start.6
  0.8 0.0 copy-start.7
  0.9 0.0 copy-start.8
  0.9 0.2 %copy-done.1 = bf16[320,1024]{1,0:T(8,128)(2,1)S(1)} copy-done((bf16[320,1024]{1,0:T(8,128)(2,1)S(1)}, bf16[320,1024]{1,0:T(8,128)(2,1)}, u32[]{:S(2)}) %copy-start.1) | copy-done | bytes 655384
  1.1 0.1 shard_map.92
  1.1 0.0 copy-start
  1.2 3.0 %collective-permute-start = (bf16[1056,128]{1,0:T(8,128)(2,1)S(1)}, bf16[1056,128]{1,0:T(8,128)(2,1)S(1)}, u32[]{:S(2)}, u32[]{:S(2)}) collective-permute-start(bf16[1056,128]{1,0:T(8,128)(2,1)S(1)} %shard_map.92), channel_id=1, source_target_pairs={{1,0},{30,31},{0,2},{3,1},{2,4},{5,3},{4,6},{7,5},{6,8},{9,7},{8,1... | collective-permute-start | bytes 811016 | tf_op jit(solution)/shard_map/ppermute | solution.py:437
  4.2 0.0 copy-done.6
  4.2 0.0 copy-done.7
  4.2 0.0 copy-done.8
  4.2 1.0 %shard_map.93 = (bf16[296,1024]{1,0:T(8,128)(2,1)S(1)}, s32[8,256]{1,0:T(8,128)S(1)}) custom-call(bf16[320,1024]{1,0:T(8,128)(2,1)S(1)} %copy-done.1, s32[320]{0:T(512)S(1)} %copy-done.8, f32[1,1024]{1,0:T(1,128)S(1)} %bitcast.8, f32[1,1024]{1,0:T(1,128)S(1)} %bitcast.10), custom_call_target="tpu_custom_call" | custom-call | flops 1500000000 | bytes 1000000 | tf_op jit(solution)/shard_map/pallas_call | solution.py:450
  5.2 0.0 copy-done
  5.2 2.2 %shard_map.94 = (bf16[168,512]{1,0:T(8,128)(2,1)S(1)}, bf16[296,512]{1,0:T(8,128)(2,1)S(1)}, bf16[296,512]{1,0:T(8,128)(2,1)S(1)}, f32[4,168,128]{2,1,0:T(8,128)...) custom-call(bf16[296,1024]{1,0:T(8,128)(2,1)S(1)} %get-tuple-element.30.normed, ...), custom_call_target="tpu_custom_call" | custom-call | flops 1300000000 | bytes 4000000 | tf_op jit(solution)/shard_map/pallas_call | solution.py:458
  7.4 0.0 collective-permute-done.2.w.refs_8_
  7.4 2.2 %shard_map.95 = (bf16[168,512]{1,0:T(8,128)(2,1)S(1)}, bf16[296,512]{1,0:T(8,128)(2,1)S(1)}, bf16[296,512]{1,0:T(8,128)(2,1)S(1)}, f32[4,168,128]{2,1,0:T(8,128)...) custom-call(bf16[296,1024]{1,0:T(8,128)(2,1)S(1)} %get-tuple-element, ...), custom_call_target="tpu_custom_call" | custom-call | flops 1300000000 | bytes 4000000 | tf_op jit(solution)/shard_map/pallas_call | solution.py:467
  9.6 1.5 %collective-permute-done.halo = bf16[1056,128]{1,0:T(8,128)(2,1)S(1)} collective-permute-done((bf16[1056,128]{1,0:T(8,128)(2,1)S(1)}, bf16[1056,128]{1,0:T(8,128)(2,1)S(1)}, u32[]{:S(2)}, u32[]{:S(2)}) %collective-permute-start) | collective-permute-done | bytes 270368 | tf_op jit(solution)/shard_map/ppermute | solution.py:437
  11.1 0.0 collective-permute-done.1.wo
  11.1 0.0 copy-start.2
  11.1 0.0 copy-start.3
  11.1 0.0 copy-start.4
  11.1 0.0 copy-start.5
  11.1 2.1 %shard_map.96 = (bf16[176,512]{1,0:T(8,128)(2,1)S(1)}, bf16[192,1024]{1,0:T(8,128)(2,1)S(1)}) custom-call(bf16[1056,128]{1,0:T(8,128)(2,1)S(1)} %collective-permute-done.halo, bf16[320,1024]{1,0:T(8,128)(2,1)S(1)} %copy-done.1, f32[1,1024]{1,0:T(1,128)S(1)} %bitcast.9, f32[1,1024]{1,0:T(1,128)S(1)} %bitcast.11, ...), custom_call_target="tpu_custom_call" | custom-call | flops 1500000000 | bytes 10000000 | tf_op jit(solution)/shard_map/pallas_call | solution.py:477
  13.2 0.1 collective-permute-start.3
  13.2 0.0 copy-done.2
  13.2 0.4 %shard_map.97.keep = bf16[176,512]{1,0:T(8,128)(2,1)S(1)} custom-call(bf16[192,1024]{1,0:T(8,128)(2,1)S(1)} %get-tuple-element.48.att_all, bf16[320,1024]{1,0:T(8,128)(2,1)S(1)} %copy-done.1, bf16[1056,128]{1,0:T(8,128)(2,1)S(1)} %collective-permute-done.halo, bf16[1024,512]{1,0:T(8,128)(2,1)S(1)} %copy-done.2), custom_call_target="tpu_custom_call" | custom-call | flops 200000000 | bytes 1000000 | tf_op jit(solution)/shard_map/pallas_call | solution.py:492
  13.6 0.0 copy-done.3
  13.7 0.0 copy-done.4
  13.7 0.0 copy-done.5
  13.7 0.5 %shard_map.98.done = bf16[160,512]{1,0:T(8,128)(2,1)S(1)} custom-call(bf16[176,512]{1,0:T(8,128)(2,1)S(1)} %shard_map.97.keep, bf16[1280,176]{1,0:T(8,128)(2,1)S(1)} %get-tuple-element.49.shift_by, f32[176,128]{1,0:T(8,128)S(1)} %get-tuple-element.50.mask, f32[9,512]{1,0:T(8,128)S(1)} %copy-done.3, f32[1,512]{1,0:T(1,128)S(1)} %bitcast.4, f32[1,512]{1,0:T(1,128)S(1)} %bitcast.6), custom_call_target="tpu_custom_call" | custom-call | flops 270000000 | bytes 1000000 | tf_op jit(solution)/shard_map/pallas_call | solution.py:501
  14.2 0.4 %collective-permute-done.3.got = bf16[176,512]{1,0:T(8,128)(2,1)S(1)} collective-permute-done((bf16[176,512]{1,0:T(8,128)(2,1)S(1)}, bf16[176,512]{1,0:T(8,128)(2,1)S(1)}, u32[]{:S(2)}, u32[]{:S(2)}) %collective-permute-start.3) | collective-permute-done | bytes 180256 | tf_op jit(solution)/shard_map/ppermute | solution.py:491
  14.6 1.2 %shard_map.99 = bf16[320,512]{1,0:T(8,128)(2,1)} custom-call(bf16[176,512]{1,0:T(8,128)(2,1)S(1)} %collective-permute-done.3.got, bf16[160,512]{1,0:T(8,128)(2,1)S(1)} %shard_map.98.done, bf16[1280,176]{1,0:T(8,128)(2,1)S(1)} %get-tuple-element.51.shift_by, f32[176,128]{1,0:T(8,128)S(1)} %get-tuple-element.52.mask, f32[9,512]{1,0:T(8,128)S(1)} %copy-done.3, ...), custom_call_target="tpu_custom_call" | custom-call | flops 270000000 | bytes 1000000 | tf_op jit(solution)/shard_map/pallas_call | solution.py:509
Async XLA Ops:
  0.0 1.1 %copy-start.1 = (bf16[320,1024]{1,0:T(8,128)(2,1)S(1)}, bf16[320,1024]{1,0:T(8,128)(2,1)}, u32[]{:S(2)}) copy-start(bf16[320,1024]{1,0:T(8,128)(2,1)} %frames.7) | copy-start | bytes 1966084
  0.0 7.4 %collective-permute-start.2 = (bf16[3,1024,512]{2,1,0:T(8,128)(2,1)}, bf16[3,1024,512]{2,1,0:T(8,128)(2,1)S(1)}, u32[]{:S(2)}, u32[]{:S(2)}) collective-permute-start(bf16[3,1024,512]{2,1,0:T(8,128)(2,1)} %refs_0_.1), channel_id=1, source_target_pairs={{0,1},{1,0},{2,3},{3,2},{4,5},{5,4},{6,7},{7,6},{8,9},{9,8},{10,11... | collective-permute-start | bytes 9437192 | tf_op jit(solution)/shard_map/ppermute | solution.py:438
  0.5 10.6 %collective-permute-start.1 = (bf16[1024,512]{1,0:T(8,128)(2,1)}, bf16[1024,512]{1,0:T(8,128)(2,1)S(1)}, u32[]{:S(2)}, u32[]{:S(2)}) collective-permute-start(bf16[1024,512]{1,0:T(8,128)(2,1)} %wo.1), channel_id=1, source_target_pairs={{0,1},{1,0},{2,3},{3,2},{4,5},{5,4},{6,7},{7,6},{8,9},{9,8},{10,11... | collective-permute-start | bytes 3145736 | tf_op jit(solution)/shard_map/ppermute | solution.py:439
  0.8 3.4 %copy-start.6 = (f32[1024]{0:T(1024)S(1)}, f32[1024]{0:T(1024)}, u32[]{:S(2)}) copy-start(f32[1024]{0:T(1024)} %param.11) | copy-start | bytes 12292
  0.8 3.3 %copy-start.7 = (f32[1024]{0:T(1024)S(1)}, f32[1024]{0:T(1024)}, u32[]{:S(2)}) copy-start(f32[1024]{0:T(1024)} %param.12) | copy-start | bytes 12292
  0.9 3.3 %copy-start.8 = (s32[320]{0:T(512)S(1)}, s32[320]{0:T(512)}, u32[]{:S(2)}) copy-start(s32[320]{0:T(512)} %valid.1) | copy-start | bytes 3844
  1.1 4.1 %copy-start = (bf16[3,1024,512]{2,1,0:T(8,128)(2,1)S(1)}, bf16[3,1024,512]{2,1,0:T(8,128)(2,1)}, u32[]{:S(2)}) copy-start(bf16[3,1024,512]{2,1,0:T(8,128)(2,1)} %refs_0_.1) | copy-start | bytes 9437188
  1.2 9.9 %collective-permute-start = (bf16[1056,128]{1,0:T(8,128)(2,1)S(1)}, bf16[1056,128]{1,0:T(8,128)(2,1)S(1)}, u32[]{:S(2)}, u32[]{:S(2)}) collective-permute-start(bf16[1056,128]{1,0:T(8,128)(2,1)S(1)} %shard_map.92), channel_id=1, source_target_pairs={{1,0},{30,31},{0,2},{3,1},{2,4},{5,3},{4,6},{7,5},{6,8},{9,7},{8,1... | collective-permute-start | bytes 811016 | tf_op jit(solution)/shard_map/ppermute | solution.py:437
  11.1 2.2 %copy-start.2 = (bf16[1024,512]{1,0:T(8,128)(2,1)S(1)}, bf16[1024,512]{1,0:T(8,128)(2,1)}, u32[]{:S(2)}) copy-start(bf16[1024,512]{1,0:T(8,128)(2,1)} %wo.1) | copy-start | bytes 3145732
  11.1 2.6 %copy-start.3 = (f32[9,512]{1,0:T(8,128)S(1)}, f32[9,512]{1,0:T(8,128)}, u32[]{:S(2)}) copy-start(f32[9,512]{1,0:T(8,128)} %weight.3) | copy-start | bytes 55300
  11.1 2.6 %copy-start.4 = (f32[512]{0:T(512)S(1)}, f32[512]{0:T(512)}, u32[]{:S(2)}) copy-start(f32[512]{0:T(512)} %param.16) | copy-start | bytes 6148
  11.1 2.6 %copy-start.5 = (f32[512]{0:T(512)S(1)}, f32[512]{0:T(512)}, u32[]{:S(2)}) copy-start(f32[512]{0:T(512)} %param.17) | copy-start | bytes 6148
  13.2 1.5 %collective-permute-start.3 = (bf16[176,512]{1,0:T(8,128)(2,1)S(1)}, bf16[176,512]{1,0:T(8,128)(2,1)S(1)}, u32[]{:S(2)}, u32[]{:S(2)}) collective-permute-start(bf16[176,512]{1,0:T(8,128)(2,1)S(1)} %get-tuple-element.47), channel_id=1, source_target_pairs={{0,1},{1,0},{2,3},{3,2},{4,5},{5,4},{6,7},{7,6},{8,9},{9,8},{10,11... | collective-permute-start | bytes 540680 | tf_op jit(solution)/shard_map/ppermute | solution.py:491
where the time goes:
time: 16 us; the launch traced here: 15.8 us
  Pallas kernels  9.89 us (62%)
  starting transfers between devices  3.65 us (23%)
  waiting for transfers between devices  1.9 us (12%)
  local copies, waits for them, and re-layouts  0.27 us (2%)
    ppermute x1, starting transfers between devices, compute(): halo = lax.ppermute(sent, ('tm', 'mp'), pairs)  3.02 us
    pallas_call x1, Pallas kernels, compute(): call(second_kernel, results + shift_shapes + (shaped((block, LANES), F32)...  2.22 us
    pallas_call x1, Pallas kernels, compute(): call(first_kernel, results, [VMEM] * 3, (VMEM,) * 7, flops=1300000000, si...  2.15 us
    pallas_call x1, Pallas kernels, compute(): call(halo_kernel, (shaped((block, width), BF16), shaped((pl.cdiv(queries,...  2.07 us
    ppermute x1, waiting for transfers between devices, compute(): halo = lax.ppermute(sent, ('tm', 'mp'), pairs)  1.46 us
    pallas_call x1, Pallas kernels, compute(): call(other_conv_kernel, shaped((rows, width), BF16), [VMEM] * 7, ANY, [pl...  1.21 us
    pallas_call x1, Pallas kernels, compute(): call(norm_kernel, (shaped((keys, model), BF16), shaped((8, 256), jnp.int3...  1 us
    pallas_call x1, Pallas kernels, compute(): call(own_conv_kernel, shaped((half, width), BF16), [VMEM] * 6, VMEM, flop...  0.53 us
  transfers between devices with their start and end apart: 4, of which 2 were waited for; matrix products, arithmetic and copies ran while one was open for 0% of the time, Pallas kernels for 42%

commit v1 on v0

--- a/solution.py
+++ b/solution.py
@@ -377,25 +377,15 @@
     convolved(keep, core, shift_by, mask, weight, scale, shift, store)
 
 
-def other_conv_kernel(got, done, shift_by, mask, weight, scale, shift, out, block, sems):
+def other_conv_kernel(got, done, shift_by, mask, weight, scale, shift, out):
     core = 1 - lax.axis_index("mp")
     half = done.shape[0]
-    first = pltpu.make_async_copy(done, out.at[rows_at((1 - core) * half, half), :], sems.at[0])
-    first.start()
-    copies = [first]
+    out[rows_at((1 - core) * half, half), :] = done[...]
 
     def store(lanes, value):
-        block[:, lanes] = value
-        copies.append(
-            pltpu.make_async_copy(
-                block.at[:, lanes], out.at[rows_at(core * half, half), lanes], sems.at[len(copies)]
-            )
-        )
-        copies[-1].start()
+        out[rows_at(core * half, half), lanes] = value
 
     convolved(got, core, shift_by, mask, weight, scale, shift, store)
-    for copy in copies:
-        copy.wait()
 
 
 def call(kernel, out_shape, in_specs, out_specs, scratch=(), flops=0, size=0, exps=0, limit=16):
@@ -510,8 +500,7 @@
         other_conv_kernel,
         shaped((rows, width), BF16),
         [VMEM] * 7,
-        ANY,
-        [pltpu.VMEM((half, width), BF16), pltpu.SemaphoreType.DMA((1 + width // 256,))],
+        VMEM,
         flops=270_000_000,
         size=1_000_000,
     )(got, done, other_shift, other_mask, *weights)

time: 16 us -> 16.1 us (level)
  no operation moved by 1% of the time
where the time goes in v1:
time: 16.1 us; the launch traced here: 15.9 us
  Pallas kernels  9.96 us (62%)
  starting transfers between devices  3.65 us (23%)
  waiting for transfers between devices  1.9 us (12%)
  local copies, waits for them, and re-layouts  0.27 us (2%)
    ppermute x1, starting transfers between devices, compute(): halo = lax.ppermute(sent, ('tm', 'mp'), pairs)  3.02 us
    pallas_call x1, Pallas kernels, compute(): call(second_kernel, results + shift_shapes + (shaped((block, LANES), F32)...  2.22 us
    pallas_call x1, Pallas kernels, compute(): call(first_kernel, results, [VMEM] * 3, (VMEM,) * 7, flops=1300000000, si...  2.15 us
    pallas_call x1, Pallas kernels, compute(): call(halo_kernel, (shaped((block, width), BF16), shaped((pl.cdiv(queries,...  2.07 us
    ppermute x1, waiting for transfers between devices, compute(): halo = lax.ppermute(sent, ('tm', 'mp'), pairs)  1.46 us
    pallas_call x1, Pallas kernels, compute(): call(other_conv_kernel, shaped((rows, width), BF16), [VMEM] * 7, VMEM, fl...  1.27 us
    pallas_call x1, Pallas kernels, compute(): call(norm_kernel, (shaped((keys, model), BF16), shaped((8, 256), jnp.int3...  1 us
    pallas_call x1, Pallas kernels, compute(): call(own_conv_kernel, shaped((half, width), BF16), [VMEM] * 6, VMEM, flop...  0.53 us
  transfers between devices with their start and end apart: 4, of which 2 were waited for; matrix products, arithmetic and copies ran while one was open for 0% of the time, Pallas kernels for 42%

profile of v1, /device:TPU:0, one launch (start us, length us, event | category | flops | bytes accessed | tf_op | source)
XLA Modules:
  0.0 15.9 jit_solution(6302857448900884283)
XLA Ops:
  0.0 0.0 copy-start.1
  0.0 0.5 %collective-permute-start.2 = (bf16[3,1024,512]{2,1,0:T(8,128)(2,1)}, bf16[3,1024,512]{2,1,0:T(8,128)(2,1)S(1)}, u32[]{:S(2)}, u32[]{:S(2)}) collective-permute-start(bf16[3,1024,512]{2,1,0:T(8,128)(2,1)} %refs_0_.1), channel_id=1, source_target_pairs={{0,1},{1,0},{2,3},{3,2},{4,5},{5,4},{6,7},{7,6},{8,9},{9,8},{10,11... | collective-permute-start | bytes 9437192 | tf_op jit(solution)/shard_map/ppermute | solution.py:428
  0.5 0.1 collective-permute-start.1
  0.6 0.3 %shard_map.91 = (bf16[1280,176]{1,0:T(8,128)(2,1)S(1)}, bf16[1280,176]{1,0:T(8,128)(2,1)S(1)}) custom-call(), custom_call_target="tpu_custom_call" | custom-call | flops 1500000000 | tf_op jit(solution)/shard_map/pallas_call | solution.py:419
  0.8 0.0 copy-start.6
  0.8 0.0 copy-start.7
  0.9 0.0 copy-start.8
  0.9 0.2 %copy-done.1 = bf16[320,1024]{1,0:T(8,128)(2,1)S(1)} copy-done((bf16[320,1024]{1,0:T(8,128)(2,1)S(1)}, bf16[320,1024]{1,0:T(8,128)(2,1)}, u32[]{:S(2)}) %copy-start.1) | copy-done | bytes 655384
  1.1 0.1 shard_map.92
  1.1 0.0 copy-start
  1.2 3.0 %collective-permute-start = (bf16[1056,128]{1,0:T(8,128)(2,1)S(1)}, bf16[1056,128]{1,0:T(8,128)(2,1)S(1)}, u32[]{:S(2)}, u32[]{:S(2)}) collective-permute-start(bf16[1056,128]{1,0:T(8,128)(2,1)S(1)} %shard_map.92), channel_id=1, source_target_pairs={{1,0},{30,31},{0,2},{3,1},{2,4},{5,3},{4,6},{7,5},{6,8},{9,7},{8,1... | collective-permute-start | bytes 811016 | tf_op jit(solution)/shard_map/ppermute | solution.py:427
  4.2 0.0 copy-done.6
  4.2 0.0 copy-done.7
  4.2 0.0 copy-done.8
  4.2 1.0 %shard_map.93 = (bf16[296,1024]{1,0:T(8,128)(2,1)S(1)}, s32[8,256]{1,0:T(8,128)S(1)}) custom-call(bf16[320,1024]{1,0:T(8,128)(2,1)S(1)} %copy-done.1, s32[320]{0:T(512)S(1)} %copy-done.8, f32[1,1024]{1,0:T(1,128)S(1)} %bitcast.8, f32[1,1024]{1,0:T(1,128)S(1)} %bitcast.10), custom_call_target="tpu_custom_call" | custom-call | flops 1500000000 | bytes 1000000 | tf_op jit(solution)/shard_map/pallas_call | solution.py:440
  5.2 0.0 copy-done
  5.2 2.2 %shard_map.94 = (bf16[168,512]{1,0:T(8,128)(2,1)S(1)}, bf16[296,512]{1,0:T(8,128)(2,1)S(1)}, bf16[296,512]{1,0:T(8,128)(2,1)S(1)}, f32[4,168,128]{2,1,0:T(8,128)...) custom-call(bf16[296,1024]{1,0:T(8,128)(2,1)S(1)} %get-tuple-element.30.normed, ...), custom_call_target="tpu_custom_call" | custom-call | flops 1300000000 | bytes 4000000 | tf_op jit(solution)/shard_map/pallas_call | solution.py:448
  7.4 0.0 collective-permute-done.2.w.refs_8_
  7.4 2.2 %shard_map.95 = (bf16[168,512]{1,0:T(8,128)(2,1)S(1)}, bf16[296,512]{1,0:T(8,128)(2,1)S(1)}, bf16[296,512]{1,0:T(8,128)(2,1)S(1)}, f32[4,168,128]{2,1,0:T(8,128)...) custom-call(bf16[296,1024]{1,0:T(8,128)(2,1)S(1)} %get-tuple-element, ...), custom_call_target="tpu_custom_call" | custom-call | flops 1300000000 | bytes 4000000 | tf_op jit(solution)/shard_map/pallas_call | solution.py:457
  9.6 1.5 %collective-permute-done.halo = bf16[1056,128]{1,0:T(8,128)(2,1)S(1)} collective-permute-done((bf16[1056,128]{1,0:T(8,128)(2,1)S(1)}, bf16[1056,128]{1,0:T(8,128)(2,1)S(1)}, u32[]{:S(2)}, u32[]{:S(2)}) %collective-permute-start) | collective-permute-done | bytes 270368 | tf_op jit(solution)/shard_map/ppermute | solution.py:427
  11.1 0.0 collective-permute-done.1.wo
  11.1 0.0 copy-start.2
  11.1 0.0 copy-start.3
  11.1 0.0 copy-start.4
  11.1 0.0 copy-start.5
  11.1 2.1 %shard_map.96 = (bf16[176,512]{1,0:T(8,128)(2,1)S(1)}, bf16[192,1024]{1,0:T(8,128)(2,1)S(1)}) custom-call(bf16[1056,128]{1,0:T(8,128)(2,1)S(1)} %collective-permute-done.halo, bf16[320,1024]{1,0:T(8,128)(2,1)S(1)} %copy-done.1, f32[1,1024]{1,0:T(1,128)S(1)} %bitcast.9, f32[1,1024]{1,0:T(1,128)S(1)} %bitcast.11, ...), custom_call_target="tpu_custom_call" | custom-call | flops 1500000000 | bytes 10000000 | tf_op jit(solution)/shard_map/pallas_call | solution.py:467
  13.2 0.1 collective-permute-start.3
  13.2 0.0 copy-done.2
  13.2 0.4 %shard_map.97.keep = bf16[176,512]{1,0:T(8,128)(2,1)S(1)} custom-call(bf16[192,1024]{1,0:T(8,128)(2,1)S(1)} %get-tuple-element.48.att_all, bf16[320,1024]{1,0:T(8,128)(2,1)S(1)} %copy-done.1, bf16[1056,128]{1,0:T(8,128)(2,1)S(1)} %collective-permute-done.halo, bf16[1024,512]{1,0:T(8,128)(2,1)S(1)} %copy-done.2), custom_call_target="tpu_custom_call" | custom-call | flops 200000000 | bytes 1000000 | tf_op jit(solution)/shard_map/pallas_call | solution.py:482
  13.6 0.0 copy-done.3
  13.7 0.0 copy-done.4
  13.7 0.0 copy-done.5
  13.7 0.5 %shard_map.98.done = bf16[160,512]{1,0:T(8,128)(2,1)S(1)} custom-call(bf16[176,512]{1,0:T(8,128)(2,1)S(1)} %shard_map.97.keep, bf16[1280,176]{1,0:T(8,128)(2,1)S(1)} %get-tuple-element.49.shift_by, f32[176,128]{1,0:T(8,128)S(1)} %get-tuple-element.50.mask, f32[9,512]{1,0:T(8,128)S(1)} %copy-done.3, f32[1,512]{1,0:T(1,128)S(1)} %bitcast.4, f32[1,512]{1,0:T(1,128)S(1)} %bitcast.6), custom_call_target="tpu_custom_call" | custom-call | flops 270000000 | bytes 1000000 | tf_op jit(solution)/shard_map/pallas_call | solution.py:491
  14.2 0.4 %collective-permute-done.3.got = bf16[176,512]{1,0:T(8,128)(2,1)S(1)} collective-permute-done((bf16[176,512]{1,0:T(8,128)(2,1)S(1)}, bf16[176,512]{1,0:T(8,128)(2,1)S(1)}, u32[]{:S(2)}, u32[]{:S(2)}) %collective-permute-start.3) | collective-permute-done | bytes 180256 | tf_op jit(solution)/shard_map/ppermute | solution.py:481
  14.6 1.3 %shard_map.99 = bf16[320,512]{1,0:T(8,128)(2,1)} custom-call(bf16[176,512]{1,0:T(8,128)(2,1)S(1)} %collective-permute-done.3.got, bf16[160,512]{1,0:T(8,128)(2,1)S(1)} %shard_map.98.done, bf16[1280,176]{1,0:T(8,128)(2,1)S(1)} %get-tuple-element.51.shift_by, f32[176,128]{1,0:T(8,128)S(1)} %get-tuple-element.52.mask, f32[9,512]{1,0:T(8,128)S(1)} %copy-done.3, ...), custom_call_target="tpu_custom_call" | custom-call | flops 270000000 | bytes 1000000 | tf_op jit(solution)/shard_map/pallas_call | solution.py:499
Async XLA Ops:
  0.0 1.1 %copy-start.1 = (bf16[320,1024]{1,0:T(8,128)(2,1)S(1)}, bf16[320,1024]{1,0:T(8,128)(2,1)}, u32[]{:S(2)}) copy-start(bf16[320,1024]{1,0:T(8,128)(2,1)} %frames.7) | copy-start | bytes 1966084
  0.0 7.4 %collective-permute-start.2 = (bf16[3,1024,512]{2,1,0:T(8,128)(2,1)}, bf16[3,1024,512]{2,1,0:T(8,128)(2,1)S(1)}, u32[]{:S(2)}, u32[]{:S(2)}) collective-permute-start(bf16[3,1024,512]{2,1,0:T(8,128)(2,1)} %refs_0_.1), channel_id=1, source_target_pairs={{0,1},{1,0},{2,3},{3,2},{4,5},{5,4},{6,7},{7,6},{8,9},{9,8},{10,11... | collective-permute-start | bytes 9437192 | tf_op jit(solution)/shard_map/ppermute | solution.py:428
  0.5 10.6 %collective-permute-start.1 = (bf16[1024,512]{1,0:T(8,128)(2,1)}, bf16[1024,512]{1,0:T(8,128)(2,1)S(1)}, u32[]{:S(2)}, u32[]{:S(2)}) collective-permute-start(bf16[1024,512]{1,0:T(8,128)(2,1)} %wo.1), channel_id=1, source_target_pairs={{0,1},{1,0},{2,3},{3,2},{4,5},{5,4},{6,7},{7,6},{8,9},{9,8},{10,11... | collective-permute-start | bytes 3145736 | tf_op jit(solution)/shard_map/ppermute | solution.py:429
  0.8 3.4 %copy-start.6 = (f32[1024]{0:T(1024)S(1)}, f32[1024]{0:T(1024)}, u32[]{:S(2)}) copy-start(f32[1024]{0:T(1024)} %param.11) | copy-start | bytes 12292
  0.8 3.3 %copy-start.7 = (f32[1024]{0:T(1024)S(1)}, f32[1024]{0:T(1024)}, u32[]{:S(2)}) copy-start(f32[1024]{0:T(1024)} %param.12) | copy-start | bytes 12292
  0.9 3.3 %copy-start.8 = (s32[320]{0:T(512)S(1)}, s32[320]{0:T(512)}, u32[]{:S(2)}) copy-start(s32[320]{0:T(512)} %valid.1) | copy-start | bytes 3844
  1.1 4.1 %copy-start = (bf16[3,1024,512]{2,1,0:T(8,128)(2,1)S(1)}, bf16[3,1024,512]{2,1,0:T(8,128)(2,1)}, u32[]{:S(2)}) copy-start(bf16[3,1024,512]{2,1,0:T(8,128)(2,1)} %refs_0_.1) | copy-start | bytes 9437188
  1.2 9.9 %collective-permute-start = (bf16[1056,128]{1,0:T(8,128)(2,1)S(1)}, bf16[1056,128]{1,0:T(8,128)(2,1)S(1)}, u32[]{:S(2)}, u32[]{:S(2)}) collective-permute-start(bf16[1056,128]{1,0:T(8,128)(2,1)S(1)} %shard_map.92), channel_id=1, source_target_pairs={{1,0},{30,31},{0,2},{3,1},{2,4},{5,3},{4,6},{7,5},{6,8},{9,7},{8,1... | collective-permute-start | bytes 811016 | tf_op jit(solution)/shard_map/ppermute | solution.py:427
  11.1 2.2 %copy-start.2 = (bf16[1024,512]{1,0:T(8,128)(2,1)S(1)}, bf16[1024,512]{1,0:T(8,128)(2,1)}, u32[]{:S(2)}) copy-start(bf16[1024,512]{1,0:T(8,128)(2,1)} %wo.1) | copy-start | bytes 3145732
  11.1 2.6 %copy-start.3 = (f32[9,512]{1,0:T(8,128)S(1)}, f32[9,512]{1,0:T(8,128)}, u32[]{:S(2)}) copy-start(f32[9,512]{1,0:T(8,128)} %weight.3) | copy-start | bytes 55300
  11.1 2.6 %copy-start.4 = (f32[512]{0:T(512)S(1)}, f32[512]{0:T(512)}, u32[]{:S(2)}) copy-start(f32[512]{0:T(512)} %param.16) | copy-start | bytes 6148
  11.1 2.6 %copy-start.5 = (f32[512]{0:T(512)S(1)}, f32[512]{0:T(512)}, u32[]{:S(2)}) copy-start(f32[512]{0:T(512)} %param.17) | copy-start | bytes 6148
  13.2 1.5 %collective-permute-start.3 = (bf16[176,512]{1,0:T(8,128)(2,1)S(1)}, bf16[176,512]{1,0:T(8,128)(2,1)S(1)}, u32[]{:S(2)}, u32[]{:S(2)}) collective-permute-start(bf16[176,512]{1,0:T(8,128)(2,1)S(1)} %get-tuple-element.47), channel_id=1, source_target_pairs={{0,1},{1,0},{2,3},{3,2},{4,5},{5,4},{6,7},{7,6},{8,9},{9,8},{10,11... | collective-permute-start | bytes 540680 | tf_op jit(solution)/shard_map/ppermute | solution.py:481

commit v2 on v0

--- a/solution.py
+++ b/solution.py
@@ -96,18 +96,22 @@
     key_pos = positions((queries, keys), 1, key_at)
     query_pos = positions((queries, keys), 0, query_at)
     allowed = (jnp.abs(key_pos - query_pos) <= CTX) & (key_pos < count)
-    for head in range(q_out.shape[1] // HEAD_DIM):
-        at = slice(head * HEAD_DIM, (head + 1) * HEAD_DIM)
-        scores = dot_t(q_out[:, at], k_out[:, at])
-        scores = jnp.where(allowed, scores, NEG)
-        top = jnp.max(scores, axis=-1, keepdims=True)
-        raised = jnp.exp2(scores - top)
-        total = jnp.sum(raised, axis=-1, keepdims=True)
+    heads = [slice(at, at + HEAD_DIM) for at in range(0, q_out.shape[1], HEAD_DIM)]
+    scores = [dot_t(q_out[:, at], k_out[:, at]) for at in heads]
+    raised, totals = [], []
+    for head, score in enumerate(scores):
+        score = jnp.where(allowed, score, NEG)
+        top = jnp.max(score, axis=-1, keepdims=True)
+        up = jnp.exp2(score - top)
+        total = jnp.sum(up, axis=-1, keepdims=True)
         top_out[head] = jnp.broadcast_to(top, (queries, HEAD_DIM))
         total_out[head] = jnp.broadcast_to(total, (queries, HEAD_DIM))
-        acc = dot(raised.astype(BF16), v_out[:, at])
+        raised.append(up.astype(BF16))
+        totals.append(total)
+    for head, at in enumerate(heads):
+        acc = dot(raised[head], v_out[:, at])
         acc_out[:, at] = acc
-        att_out[:, at] = (acc * (1.0 / total)).astype(BF16)
+        att_out[:, at] = (acc * (1.0 / totals[head])).astype(BF16)
 
 
 def norm_kernel(frames, valid, gain, bias, normed, count_here):

time: 16 us -> 16 us (level)
  Pallas kernels: 9.89 us -> 8.64 us
  waiting for transfers between devices: 1.9 us -> 3.14 us
    ppermute x1, waiting for transfers between devices: 1.46 us -> 2.7 us  [compute(): halo = lax.ppermute(sent, ('tm', 'mp'), pairs)]
    pallas_call x1, Pallas kernels: 2.15 us -> 1.48 us  [compute(): call(first_kernel, results, [VMEM] * 3, (VMEM,) * 7, flops=1300000000, si...]
    pallas_call x1, Pallas kernels: 2.22 us -> 1.65 us  [compute(): call(second_kernel, results + shift_shapes + (shaped((block, LANES), F32)...]
  transfers between devices with their start and end apart: 4 -> 4, of which waited for: 2 -> 2; matrix products, arithmetic and copies ran while one was open for 0% -> 0% of each run, Pallas kernels for 42% -> 34%
where the time goes in v2:
time: 16 us; the launch traced here: 15.8 us
  Pallas kernels  8.64 us (54%)
  starting transfers between devices  3.65 us (23%)
  waiting for transfers between devices  3.14 us (20%)
  local copies, waits for them, and re-layouts  0.27 us (2%)
    ppermute x1, starting transfers between devices, compute(): halo = lax.ppermute(sent, ('tm', 'mp'), pairs)  3.02 us
    ppermute x1, waiting for transfers between devices, compute(): halo = lax.ppermute(sent, ('tm', 'mp'), pairs)  2.7 us
    pallas_call x1, Pallas kernels, compute(): call(halo_kernel, (shaped((block, width), BF16), shaped((pl.cdiv(queries,...  2.07 us
    pallas_call x1, Pallas kernels, compute(): call(second_kernel, results + shift_shapes + (shaped((block, LANES), F32)...  1.65 us
    pallas_call x1, Pallas kernels, compute(): call(first_kernel, results, [VMEM] * 3, (VMEM,) * 7, flops=1300000000, si...  1.48 us
    pallas_call x1, Pallas kernels, compute(): call(other_conv_kernel, shaped((rows, width), BF16), [VMEM] * 7, ANY, [pl...  1.21 us
    pallas_call x1, Pallas kernels, compute(): call(norm_kernel, (shaped((keys, model), BF16), shaped((8, 256), jnp.int3...  1 us
    pallas_call x1, Pallas kernels, compute(): call(own_conv_kernel, shaped((half, width), BF16), [VMEM] * 6, VMEM, flop...  0.53 us
  transfers between devices with their start and end apart: 4, of which 2 were waited for; matrix products, arithmetic and copies ran while one was open for 0% of the time, Pallas kernels for 34%

profile of v2, /device:TPU:0, one launch (start us, length us, event | category | flops | bytes accessed | tf_op | source)
XLA Modules:
  0.0 15.8 jit_solution(17092072225346686060)
XLA Ops:
  0.0 0.0 copy-start.1
  0.0 0.5 %collective-permute-start.2 = (bf16[3,1024,512]{2,1,0:T(8,128)(2,1)}, bf16[3,1024,512]{2,1,0:T(8,128)(2,1)S(1)}, u32[]{:S(2)}, u32[]{:S(2)}) collective-permute-start(bf16[3,1024,512]{2,1,0:T(8,128)(2,1)} %refs_0_.1), channel_id=1, source_target_pairs={{0,1},{1,0},{2,3},{3,2},{4,5},{5,4},{6,7},{7,6},{8,9},{9,8},{10,11... | collective-permute-start | bytes 9437192 | tf_op jit(solution)/shard_map/ppermute | solution.py:442
  0.5 0.1 collective-permute-start.1
  0.6 0.3 %shard_map.91 = (bf16[1280,176]{1,0:T(8,128)(2,1)S(1)}, bf16[1280,176]{1,0:T(8,128)(2,1)S(1)}) custom-call(), custom_call_target="tpu_custom_call" | custom-call | flops 1500000000 | tf_op jit(solution)/shard_map/pallas_call | solution.py:433
  0.8 0.0 copy-start.6
  0.8 0.0 copy-start.7
  0.9 0.0 copy-start.8
  0.9 0.2 %copy-done.1 = bf16[320,1024]{1,0:T(8,128)(2,1)S(1)} copy-done((bf16[320,1024]{1,0:T(8,128)(2,1)S(1)}, bf16[320,1024]{1,0:T(8,128)(2,1)}, u32[]{:S(2)}) %copy-start.1) | copy-done | bytes 655384
  1.1 0.1 shard_map.92
  1.1 0.0 copy-start
  1.2 3.0 %collective-permute-start = (bf16[1056,128]{1,0:T(8,128)(2,1)S(1)}, bf16[1056,128]{1,0:T(8,128)(2,1)S(1)}, u32[]{:S(2)}, u32[]{:S(2)}) collective-permute-start(bf16[1056,128]{1,0:T(8,128)(2,1)S(1)} %shard_map.92), channel_id=1, source_target_pairs={{1,0},{30,31},{0,2},{3,1},{2,4},{5,3},{4,6},{7,5},{6,8},{9,7},{8,1... | collective-permute-start | bytes 811016 | tf_op jit(solution)/shard_map/ppermute | solution.py:441
  4.2 0.0 copy-done.6
  4.2 0.0 copy-done.7
  4.2 0.0 copy-done.8
  4.2 1.0 %shard_map.93 = (bf16[296,1024]{1,0:T(8,128)(2,1)S(1)}, s32[8,256]{1,0:T(8,128)S(1)}) custom-call(bf16[320,1024]{1,0:T(8,128)(2,1)S(1)} %copy-done.1, s32[320]{0:T(512)S(1)} %copy-done.8, f32[1,1024]{1,0:T(1,128)S(1)} %bitcast.8, f32[1,1024]{1,0:T(1,128)S(1)} %bitcast.10), custom_call_target="tpu_custom_call" | custom-call | flops 1500000000 | bytes 1000000 | tf_op jit(solution)/shard_map/pallas_call | solution.py:454
  5.2 0.0 copy-done
  5.2 1.5 %shard_map.94 = (bf16[168,512]{1,0:T(8,128)(2,1)S(1)}, bf16[296,512]{1,0:T(8,128)(2,1)S(1)}, bf16[296,512]{1,0:T(8,128)(2,1)S(1)}, f32[4,168,128]{2,1,0:T(8,128)...) custom-call(bf16[296,1024]{1,0:T(8,128)(2,1)S(1)} %get-tuple-element.30.normed, ...), custom_call_target="tpu_custom_call" | custom-call | flops 1300000000 | bytes 4000000 | tf_op jit(solution)/shard_map/pallas_call | solution.py:462
  6.7 0.0 collective-permute-done.2.w.refs_8_
  6.7 1.6 %shard_map.95 = (bf16[168,512]{1,0:T(8,128)(2,1)S(1)}, bf16[296,512]{1,0:T(8,128)(2,1)S(1)}, bf16[296,512]{1,0:T(8,128)(2,1)S(1)}, f32[4,168,128]{2,1,0:T(8,128)...) custom-call(bf16[296,1024]{1,0:T(8,128)(2,1)S(1)} %get-tuple-element, ...), custom_call_target="tpu_custom_call" | custom-call | flops 1300000000 | bytes 4000000 | tf_op jit(solution)/shard_map/pallas_call | solution.py:471
  8.4 2.7 %collective-permute-done.halo = bf16[1056,128]{1,0:T(8,128)(2,1)S(1)} collective-permute-done((bf16[1056,128]{1,0:T(8,128)(2,1)S(1)}, bf16[1056,128]{1,0:T(8,128)(2,1)S(1)}, u32[]{:S(2)}, u32[]{:S(2)}) %collective-permute-start) | collective-permute-done | bytes 270368 | tf_op jit(solution)/shard_map/ppermute | solution.py:441
  11.1 0.0 collective-permute-done.1.wo
  11.1 0.0 copy-start.2
  11.1 0.0 copy-start.3
  11.1 0.0 copy-start.4
  11.1 0.0 copy-start.5
  11.1 2.1 %shard_map.96 = (bf16[176,512]{1,0:T(8,128)(2,1)S(1)}, bf16[192,1024]{1,0:T(8,128)(2,1)S(1)}) custom-call(bf16[1056,128]{1,0:T(8,128)(2,1)S(1)} %collective-permute-done.halo, bf16[320,1024]{1,0:T(8,128)(2,1)S(1)} %copy-done.1, f32[1,1024]{1,0:T(1,128)S(1)} %bitcast.9, f32[1,1024]{1,0:T(1,128)S(1)} %bitcast.11, ...), custom_call_target="tpu_custom_call" | custom-call | flops 1500000000 | bytes 10000000 | tf_op jit(solution)/shard_map/pallas_call | solution.py:481
  13.2 0.1 collective-permute-start.3
  13.2 0.0 copy-done.2
  13.2 0.4 %shard_map.97.keep = bf16[176,512]{1,0:T(8,128)(2,1)S(1)} custom-call(bf16[192,1024]{1,0:T(8,128)(2,1)S(1)} %get-tuple-element.48.att_all, bf16[320,1024]{1,0:T(8,128)(2,1)S(1)} %copy-done.1, bf16[1056,128]{1,0:T(8,128)(2,1)S(1)} %collective-permute-done.halo, bf16[1024,512]{1,0:T(8,128)(2,1)S(1)} %copy-done.2), custom_call_target="tpu_custom_call" | custom-call | flops 200000000 | bytes 1000000 | tf_op jit(solution)/shard_map/pallas_call | solution.py:496
  13.6 0.0 copy-done.3
  13.7 0.0 copy-done.4
  13.7 0.0 copy-done.5
  13.7 0.5 %shard_map.98.done = bf16[160,512]{1,0:T(8,128)(2,1)S(1)} custom-call(bf16[176,512]{1,0:T(8,128)(2,1)S(1)} %shard_map.97.keep, bf16[1280,176]{1,0:T(8,128)(2,1)S(1)} %get-tuple-element.49.shift_by, f32[176,128]{1,0:T(8,128)S(1)} %get-tuple-element.50.mask, f32[9,512]{1,0:T(8,128)S(1)} %copy-done.3, f32[1,512]{1,0:T(1,128)S(1)} %bitcast.4, f32[1,512]{1,0:T(1,128)S(1)} %bitcast.6), custom_call_target="tpu_custom_call" | custom-call | flops 270000000 | bytes 1000000 | tf_op jit(solution)/shard_map/pallas_call | solution.py:505
  14.2 0.4 %collective-permute-done.3.got = bf16[176,512]{1,0:T(8,128)(2,1)S(1)} collective-permute-done((bf16[176,512]{1,0:T(8,128)(2,1)S(1)}, bf16[176,512]{1,0:T(8,128)(2,1)S(1)}, u32[]{:S(2)}, u32[]{:S(2)}) %collective-permute-start.3) | collective-permute-done | bytes 180256 | tf_op jit(solution)/shard_map/ppermute | solution.py:495
  14.6 1.2 %shard_map.99 = bf16[320,512]{1,0:T(8,128)(2,1)} custom-call(bf16[176,512]{1,0:T(8,128)(2,1)S(1)} %collective-permute-done.3.got, bf16[160,512]{1,0:T(8,128)(2,1)S(1)} %shard_map.98.done, bf16[1280,176]{1,0:T(8,128)(2,1)S(1)} %get-tuple-element.51.shift_by, f32[176,128]{1,0:T(8,128)S(1)} %get-tuple-element.52.mask, f32[9,512]{1,0:T(8,128)S(1)} %copy-done.3, ...), custom_call_target="tpu_custom_call" | custom-call | flops 270000000 | bytes 1000000 | tf_op jit(solution)/shard_map/pallas_call | solution.py:513
Async XLA Ops:
  0.0 1.1 %copy-start.1 = (bf16[320,1024]{1,0:T(8,128)(2,1)S(1)}, bf16[320,1024]{1,0:T(8,128)(2,1)}, u32[]{:S(2)}) copy-start(bf16[320,1024]{1,0:T(8,128)(2,1)} %frames.7) | copy-start | bytes 1966084
  0.0 6.7 %collective-permute-start.2 = (bf16[3,1024,512]{2,1,0:T(8,128)(2,1)}, bf16[3,1024,512]{2,1,0:T(8,128)(2,1)S(1)}, u32[]{:S(2)}, u32[]{:S(2)}) collective-permute-start(bf16[3,1024,512]{2,1,0:T(8,128)(2,1)} %refs_0_.1), channel_id=1, source_target_pairs={{0,1},{1,0},{2,3},{3,2},{4,5},{5,4},{6,7},{7,6},{8,9},{9,8},{10,11... | collective-permute-start | bytes 9437192 | tf_op jit(solution)/shard_map/ppermute | solution.py:442
  0.5 10.6 %collective-permute-start.1 = (bf16[1024,512]{1,0:T(8,128)(2,1)}, bf16[1024,512]{1,0:T(8,128)(2,1)S(1)}, u32[]{:S(2)}, u32[]{:S(2)}) collective-permute-start(bf16[1024,512]{1,0:T(8,128)(2,1)} %wo.1), channel_id=1, source_target_pairs={{0,1},{1,0},{2,3},{3,2},{4,5},{5,4},{6,7},{7,6},{8,9},{9,8},{10,11... | collective-permute-start | bytes 3145736 | tf_op jit(solution)/shard_map/ppermute | solution.py:443
  0.8 3.4 %copy-start.6 = (f32[1024]{0:T(1024)S(1)}, f32[1024]{0:T(1024)}, u32[]{:S(2)}) copy-start(f32[1024]{0:T(1024)} %param.11) | copy-start | bytes 12292
  0.8 3.3 %copy-start.7 = (f32[1024]{0:T(1024)S(1)}, f32[1024]{0:T(1024)}, u32[]{:S(2)}) copy-start(f32[1024]{0:T(1024)} %param.12) | copy-start | bytes 12292
  0.9 3.3 %copy-start.8 = (s32[320]{0:T(512)S(1)}, s32[320]{0:T(512)}, u32[]{:S(2)}) copy-start(s32[320]{0:T(512)} %valid.1) | copy-start | bytes 3844
  1.1 4.1 %copy-start = (bf16[3,1024,512]{2,1,0:T(8,128)(2,1)S(1)}, bf16[3,1024,512]{2,1,0:T(8,128)(2,1)}, u32[]{:S(2)}) copy-start(bf16[3,1024,512]{2,1,0:T(8,128)(2,1)} %refs_0_.1) | copy-start | bytes 9437188
  1.2 9.9 %collective-permute-start = (bf16[1056,128]{1,0:T(8,128)(2,1)S(1)}, bf16[1056,128]{1,0:T(8,128)(2,1)S(1)}, u32[]{:S(2)}, u32[]{:S(2)}) collective-permute-start(bf16[1056,128]{1,0:T(8,128)(2,1)S(1)} %shard_map.92), channel_id=1, source_target_pairs={{1,0},{30,31},{0,2},{3,1},{2,4},{5,3},{4,6},{7,5},{6,8},{9,7},{8,1... | collective-permute-start | bytes 811016 | tf_op jit(solution)/shard_map/ppermute | solution.py:441
  11.1 2.2 %copy-start.2 = (bf16[1024,512]{1,0:T(8,128)(2,1)S(1)}, bf16[1024,512]{1,0:T(8,128)(2,1)}, u32[]{:S(2)}) copy-start(bf16[1024,512]{1,0:T(8,128)(2,1)} %wo.1) | copy-start | bytes 3145732
  11.1 2.6 %copy-start.3 = (f32[9,512]{1,0:T(8,128)S(1)}, f32[9,512]{1,0:T(8,128)}, u32[]{:S(2)}) copy-start(f32[9,512]{1,0:T(8,128)} %weight.3) | copy-start | bytes 55300
  11.1 2.6 %copy-start.4 = (f32[512]{0:T(512)S(1)}, f32[512]{0:T(512)}, u32[]{:S(2)}) copy-start(f32[512]{0:T(512)} %param.16) | copy-start | bytes 6148
  11.1 2.6 %copy-start.5 = (f32[512]{0:T(512)S(1)}, f32[512]{0:T(512)}, u32[]{:S(2)}) copy-start(f32[512]{0:T(512)} %param.17) | copy-start | bytes 6148
  13.2 1.5 %collective-permute-start.3 = (bf16[176,512]{1,0:T(8,128)(2,1)S(1)}, bf16[176,512]{1,0:T(8,128)(2,1)S(1)}, u32[]{:S(2)}, u32[]{:S(2)}) collective-permute-start(bf16[176,512]{1,0:T(8,128)(2,1)S(1)} %get-tuple-element.47), channel_id=1, source_target_pairs={{0,1},{1,0},{2,3},{3,2},{4,5},{5,4},{6,7},{7,6},{8,9},{9,8},{10,11... | collective-permute-start | bytes 540680 | tf_op jit(solution)/shard_map/ppermute | solution.py:495

commit v3 on v2

--- a/solution.py
+++ b/solution.py
@@ -84,7 +84,9 @@
     )
 
 
-def own_heads(normed, w, count, q_out, k_out, v_out, top_out, total_out, acc_out, att_out):
+def own_heads(
+    normed, w, count, q_out, k_out, v_out, top_out, total_out, acc_out, att_out, edge_out
+):
     p = lax.axis_index("mp")
     keys, queries = k_out.shape[0], q_out.shape[0]
     rows = 2 * (queries - EXT)
@@ -93,6 +95,8 @@
     picked = normed[pl.ds(pl.multiple_of(p * (keys - queries), 16), queries), :]
     q_out[...] = (dot(picked, w[0]) * SCALE).astype(BF16)
     v_out[...] = dot(normed[...], w[2]).astype(BF16)
+    edge = k_out[rows_at(p * (keys - CTX), CTX), :].astype(F32)
+    edge_out[...] = edge.T.astype(BF16)
     key_pos = positions((queries, keys), 1, key_at)
     query_pos = positions((queries, keys), 0, query_at)
     allowed = (jnp.abs(key_pos - query_pos) <= CTX) & (key_pos < count)
@@ -128,10 +132,10 @@
     norm_rows(frames, p * (rows - keys), normed, 0, keys, gain[...], bias[...])
 
 
-def first_kernel(normed, w, count_here, q, k, v, top, total, acc, att):
+def first_kernel(normed, w, count_here, q, k, v, top, total, acc, att, edge):
     keys = k.shape[0]
     count = jnp.concatenate([count_here[0:1, :]] * pl.cdiv(keys, count_here.shape[1]), axis=1)[:, :keys]
-    own_heads(normed, w, count, q, k, v, top, total, acc, att)
+    own_heads(normed, w, count, q, k, v, top, total, acc, att, edge)
 
 
 def block_time(index, core, queries, rows):
@@ -182,20 +186,21 @@
     total,
     acc,
     att,
+    edge,
     own_shift,
     other_shift,
     own_mask,
     other_mask,
 ):
     p = lax.axis_index("mp")
-    first_kernel(normed, w, count_here, q, k, v, top, total, acc, att)
+    first_kernel(normed, w, count_here, q, k, v, top, total, acc, att, edge)
     mask_shift(own_base, p, count_here, own_shift, own_mask)
     mask_shift(other_base, 1 - p, count_here, other_shift, other_mask)
 
 
 def halo_kernel(halo, frames, gain, bias, wo, *refs):
-    parts = (refs[:8], refs[8:16])
-    send, att_all, normed, kx, vx = refs[16:]
+    parts = (refs[:9], refs[9:18])
+    send, att_all, normed, kx, vx = refs[18:]
     p = lax.axis_index("mp")
     last = lax.axis_size("tm") - 1
     tm = lax.axis_index("tm")
@@ -250,10 +255,9 @@
     def lanes_of(side, at):
         return slice(side * width + at.start, side * width + at.stop)
 
-    for side, (w, q, k, v, top_own, total_own, acc_own, att) in enumerate(parts):
+    for side, (w, q, k, v, top_own, total_own, acc_own, att, edge) in enumerate(parts):
         to = slice(side * width, (side + 1) * width)
-        kx[CTX + PAD :, to] = k[own, :]
-        vx[CTX + PAD :, to] = v[own, :]
+        vx[:CTX, to] = v[own, :]
         att_all[CTX + PAD : CTX + PAD + queries - CTX, to] = att[rest, :]
 
     def project(x, i, sides):
@@ -261,8 +265,9 @@
             w = parts[side][0]
             to = slice(side * width, (side + 1) * width)
             got = dot(normed[...], w[i])
-            x[:CTX, to] = got[:CTX].astype(BF16)
-            x[CTX : CTX + PAD, to] = jnp.concatenate([got[CTX:], blank], axis=0).astype(BF16)
+            base = x.shape[0] - CTX - PAD
+            x[base : base + CTX, to] = got[:CTX].astype(BF16)
+            x[base + CTX :, to] = jnp.concatenate([got[CTX:], blank], axis=0).astype(BF16)
 
     scores = []
     project(kx, 1, (0, 1))
@@ -278,7 +283,8 @@
     scores += [
         dot_t(parts[i][1][part, at], kx[:CTX, lanes_of(i, at)]) for i, head, at in each if i == 1
     ]
-    ext_scores = dot_t(tiled, kx[...])
+    edges = jnp.concatenate([part[8][...] for part in parts], axis=0)
+    ext_scores = jnp.concatenate([dot(tiled, edges), dot_t(tiled, kx[...])], axis=1)
     project(vx, 2, (1,))
     raised, total, faded = [], [], []
     for (side, head, at), score in zip(each, scores):
@@ -295,16 +301,16 @@
     column = positions((deep, SPAN), 1, 0)
     key_pos = jnp.where(
         column < CTX,
-        column + near_at,
-        jnp.where(column < CTX + FAR, column - CTX + far_at, column - (CTX + PAD) + own_pos),
+        column + own_pos,
+        jnp.where(column < 2 * CTX, column - CTX + near_at, column - 2 * CTX + far_at),
     )
     row_pos = positions((deep, SPAN), 0, 0) % EXT + ext_at
-    seen = (jnp.abs(key_pos - row_pos) <= CTX) & ((column < CTX + FAR) | (column >= CTX + PAD))
+    seen = (jnp.abs(key_pos - row_pos) <= CTX) & (column < 2 * CTX + FAR)
     ext_scores = jnp.where(seen, ext_scores, NEG)
     ext_up = jnp.exp2(ext_scores - jnp.max(ext_scores, axis=-1, keepdims=True))
     ext_total = jnp.sum(ext_up, axis=-1, keepdims=True)
     gathered = [
-        dot(up, vx[:CTX, lanes_of(side, at)]) for (side, head, at), up in zip(each, raised)
+        dot(up, vx[CTX : 2 * CTX, lanes_of(side, at)]) for (side, head, at), up in zip(each, raised)
     ]
     spread = dot(ext_up.astype(BF16), vx[...]) * (1.0 / ext_total)
     for i, (side, head, at) in enumerate(each):
@@ -450,6 +456,7 @@
         shaped((heads, queries, HEAD_DIM), F32),
         shaped((queries, width), F32),
         shaped((queries, width), BF16),
+        shaped((width, CTX), BF16),
     )
     normed, count_here = call(
         norm_kernel,
@@ -463,7 +470,7 @@
         first_kernel,
         results,
         [VMEM] * 3,
-        (VMEM,) * 7,
+        (VMEM,) * 8,
         flops=1_300_000_000,
         size=4_000_000,
         exps=300_000,
@@ -472,20 +479,20 @@
         second_kernel,
         results + shift_shapes + (shaped((block, LANES), F32),) * 2,
         [VMEM] * 5,
-        (VMEM,) * 11,
+        (VMEM,) * 12,
         flops=1_300_000_000,
         size=4_000_000,
         exps=300_000,
     )(normed, w_other, count_here, *shifts)
-    theirs, (own_shift, other_shift, own_mask, other_mask) = second[:7], second[7:]
+    theirs, (own_shift, other_shift, own_mask, other_mask) = second[:8], second[8:]
     send, att_all = call(
         halo_kernel,
         (shaped((block, width), BF16), shaped((pl.cdiv(queries, 16) * 16 + PAD, model), BF16)),
-        [VMEM] * 21,
+        [VMEM] * 23,
         (VMEM,) * 2,
         [
             pltpu.VMEM((HALO, model), BF16),
-            pltpu.VMEM((SPAN, model), BF16),
+            pltpu.VMEM((CTX + PAD, model), BF16),
             pltpu.VMEM((SPAN, model), BF16),
         ],
         flops=1_500_000_000,

time: 16 us -> 16.1 us (level)
  no operation moved by 1% of the time
where the time goes in v3:
time: 16.1 us; the launch traced here: 15.9 us
  Pallas kernels  8.77 us (54%)
  starting transfers between devices  3.65 us (23%)
  waiting for transfers between devices  3.07 us (19%)
  local copies, waits for them, and re-layouts  0.27 us (2%)
    ppermute x1, starting transfers between devices, compute(): halo = lax.ppermute(sent, ('tm', 'mp'), pairs)  3.02 us
    ppermute x1, waiting for transfers between devices, compute(): halo = lax.ppermute(sent, ('tm', 'mp'), pairs)  2.62 us
    pallas_call x1, Pallas kernels, compute(): call(halo_kernel, (shaped((block, width), BF16), shaped((pl.cdiv(queries,...  2.12 us
    pallas_call x1, Pallas kernels, compute(): call(second_kernel, results + shift_shapes + (shaped((block, LANES), F32)...  1.69 us
    pallas_call x1, Pallas kernels, compute(): call(first_kernel, results, [VMEM] * 3, (VMEM,) * 8, flops=1300000000, si...  1.51 us
    pallas_call x1, Pallas kernels, compute(): call(other_conv_kernel, shaped((rows, width), BF16), [VMEM] * 7, ANY, [pl...  1.21 us
    pallas_call x1, Pallas kernels, compute(): call(norm_kernel, (shaped((keys, model), BF16), shaped((8, 256), jnp.int3...  1 us
    pallas_call x1, Pallas kernels, compute(): call(own_conv_kernel, shaped((half, width), BF16), [VMEM] * 6, VMEM, flop...  0.53 us
  transfers between devices with their start and end apart: 4, of which 2 were waited for; matrix products, arithmetic and copies ran while one was open for 0% of the time, Pallas kernels for 34%

profile of v3, /device:TPU:0, one launch (start us, length us, event | category | flops | bytes accessed | tf_op | source)
XLA Modules:
  0.0 15.9 jit_solution(2504058693005489672)
XLA Ops:
  0.0 0.0 copy-start.1
  0.0 0.5 %collective-permute-start.2 = (bf16[3,1024,512]{2,1,0:T(8,128)(2,1)}, bf16[3,1024,512]{2,1,0:T(8,128)(2,1)S(1)}, u32[]{:S(2)}, u32[]{:S(2)}) collective-permute-start(bf16[3,1024,512]{2,1,0:T(8,128)(2,1)} %refs_0_.1), channel_id=1, source_target_pairs={{0,1},{1,0},{2,3},{3,2},{4,5},{5,4},{6,7},{7,6},{8,9},{9,8},{10,11... | collective-permute-start | bytes 9437192 | tf_op jit(solution)/shard_map/ppermute | solution.py:448
  0.5 0.1 collective-permute-start.1
  0.6 0.3 %shard_map.91 = (bf16[1280,176]{1,0:T(8,128)(2,1)S(1)}, bf16[1280,176]{1,0:T(8,128)(2,1)S(1)}) custom-call(), custom_call_target="tpu_custom_call" | custom-call | flops 1500000000 | tf_op jit(solution)/shard_map/pallas_call | solution.py:439
  0.8 0.0 copy-start.6
  0.8 0.0 copy-start.7
  0.9 0.0 copy-start.8
  0.9 0.2 %copy-done.1 = bf16[320,1024]{1,0:T(8,128)(2,1)S(1)} copy-done((bf16[320,1024]{1,0:T(8,128)(2,1)S(1)}, bf16[320,1024]{1,0:T(8,128)(2,1)}, u32[]{:S(2)}) %copy-start.1) | copy-done | bytes 655384
  1.1 0.1 shard_map.92
  1.1 0.0 copy-start
  1.2 3.0 %collective-permute-start = (bf16[1056,128]{1,0:T(8,128)(2,1)S(1)}, bf16[1056,128]{1,0:T(8,128)(2,1)S(1)}, u32[]{:S(2)}, u32[]{:S(2)}) collective-permute-start(bf16[1056,128]{1,0:T(8,128)(2,1)S(1)} %shard_map.92), channel_id=1, source_target_pairs={{1,0},{30,31},{0,2},{3,1},{2,4},{5,3},{4,6},{7,5},{6,8},{9,7},{8,1... | collective-permute-start | bytes 811016 | tf_op jit(solution)/shard_map/ppermute | solution.py:447
  4.2 0.0 copy-done.6
  4.2 0.0 copy-done.7
  4.2 0.0 copy-done.8
  4.2 1.0 %shard_map.93 = (bf16[296,1024]{1,0:T(8,128)(2,1)S(1)}, s32[8,256]{1,0:T(8,128)S(1)}) custom-call(bf16[320,1024]{1,0:T(8,128)(2,1)S(1)} %copy-done.1, s32[320]{0:T(512)S(1)} %copy-done.8, f32[1,1024]{1,0:T(1,128)S(1)} %bitcast.8, f32[1,1024]{1,0:T(1,128)S(1)} %bitcast.10), custom_call_target="tpu_custom_call" | custom-call | flops 1500000000 | bytes 1000000 | tf_op jit(solution)/shard_map/pallas_call | solution.py:461
  5.2 0.0 copy-done
  5.2 1.5 %shard_map.94 = (bf16[168,512]{1,0:T(8,128)(2,1)S(1)}, bf16[296,512]{1,0:T(8,128)(2,1)S(1)}, bf16[296,512]{1,0:T(8,128)(2,1)S(1)}, f32[4,168,128]{2,1,0:T(8,128)...) custom-call(bf16[296,1024]{1,0:T(8,128)(2,1)S(1)} %get-tuple-element, ...), custom_call_target="tpu_custom_call" | custom-call | flops 1300000000 | bytes 4000000 | tf_op jit(solution)/shard_map/pallas_call | solution.py:469
  6.7 0.0 collective-permute-done.2.w.refs_9_
  6.7 1.7 %shard_map.95 = (bf16[168,512]{1,0:T(8,128)(2,1)S(1)}, bf16[296,512]{1,0:T(8,128)(2,1)S(1)}, bf16[296,512]{1,0:T(8,128)(2,1)S(1)}, f32[4,168,128]{2,1,0:T(8,128)...) custom-call(bf16[296,1024]{1,0:T(8,128)(2,1)S(1)} %get-tuple-element, ...), custom_call_target="tpu_custom_call" | custom-call | flops 1300000000 | bytes 4000000 | tf_op jit(solution)/shard_map/pallas_call | solution.py:478
  8.4 2.6 %collective-permute-done.halo = bf16[1056,128]{1,0:T(8,128)(2,1)S(1)} collective-permute-done((bf16[1056,128]{1,0:T(8,128)(2,1)S(1)}, bf16[1056,128]{1,0:T(8,128)(2,1)S(1)}, u32[]{:S(2)}, u32[]{:S(2)}) %collective-permute-start) | collective-permute-done | bytes 270368 | tf_op jit(solution)/shard_map/ppermute | solution.py:447
  11.1 0.0 collective-permute-done.1.wo
  11.1 0.0 copy-start.2
  11.1 0.0 copy-start.3
  11.1 0.0 copy-start.4
  11.1 0.0 copy-start.5
  11.1 2.1 %shard_map.96 = (bf16[176,512]{1,0:T(8,128)(2,1)S(1)}, bf16[192,1024]{1,0:T(8,128)(2,1)S(1)}) custom-call(bf16[1056,128]{1,0:T(8,128)(2,1)S(1)} %collective-permute-done.halo, bf16[320,1024]{1,0:T(8,128)(2,1)S(1)} %copy-done.1, f32[1,1024]{1,0:T(1,128)S(1)} %bitcast.9, f32[1,1024]{1,0:T(1,128)S(1)} %bitcast.11, ...), custom_call_target="tpu_custom_call" | custom-call | flops 1500000000 | bytes 10000000 | tf_op jit(solution)/shard_map/pallas_call | solution.py:488
  13.2 0.1 collective-permute-start.3
  13.3 0.0 copy-done.2
  13.3 0.4 %shard_map.97.keep = bf16[176,512]{1,0:T(8,128)(2,1)S(1)} custom-call(bf16[192,1024]{1,0:T(8,128)(2,1)S(1)} %get-tuple-element.52.att_all, bf16[320,1024]{1,0:T(8,128)(2,1)S(1)} %copy-done.1, bf16[1056,128]{1,0:T(8,128)(2,1)S(1)} %collective-permute-done.halo, bf16[1024,512]{1,0:T(8,128)(2,1)S(1)} %copy-done.2), custom_call_target="tpu_custom_call" | custom-call | flops 200000000 | bytes 1000000 | tf_op jit(solution)/shard_map/pallas_call | solution.py:503
  13.7 0.0 copy-done.3
  13.7 0.0 copy-done.4
  13.7 0.0 copy-done.5
  13.7 0.5 %shard_map.98.done = bf16[160,512]{1,0:T(8,128)(2,1)S(1)} custom-call(bf16[176,512]{1,0:T(8,128)(2,1)S(1)} %shard_map.97.keep, bf16[1280,176]{1,0:T(8,128)(2,1)S(1)} %get-tuple-element.53.shift_by, f32[176,128]{1,0:T(8,128)S(1)} %get-tuple-element.54.mask, f32[9,512]{1,0:T(8,128)S(1)} %copy-done.3, f32[1,512]{1,0:T(1,128)S(1)} %bitcast.4, f32[1,512]{1,0:T(1,128)S(1)} %bitcast.6), custom_call_target="tpu_custom_call" | custom-call | flops 270000000 | bytes 1000000 | tf_op jit(solution)/shard_map/pallas_call | solution.py:512
  14.3 0.4 %collective-permute-done.3.got = bf16[176,512]{1,0:T(8,128)(2,1)S(1)} collective-permute-done((bf16[176,512]{1,0:T(8,128)(2,1)S(1)}, bf16[176,512]{1,0:T(8,128)(2,1)S(1)}, u32[]{:S(2)}, u32[]{:S(2)}) %collective-permute-start.3) | collective-permute-done | bytes 180256 | tf_op jit(solution)/shard_map/ppermute | solution.py:502
  14.7 1.2 %shard_map.99 = bf16[320,512]{1,0:T(8,128)(2,1)} custom-call(bf16[176,512]{1,0:T(8,128)(2,1)S(1)} %collective-permute-done.3.got, bf16[160,512]{1,0:T(8,128)(2,1)S(1)} %shard_map.98.done, bf16[1280,176]{1,0:T(8,128)(2,1)S(1)} %get-tuple-element.55.shift_by, f32[176,128]{1,0:T(8,128)S(1)} %get-tuple-element.56.mask, f32[9,512]{1,0:T(8,128)S(1)} %copy-done.3, ...), custom_call_target="tpu_custom_call" | custom-call | flops 270000000 | bytes 1000000 | tf_op jit(solution)/shard_map/pallas_call | solution.py:520
Async XLA Ops:
  0.0 1.1 %copy-start.1 = (bf16[320,1024]{1,0:T(8,128)(2,1)S(1)}, bf16[320,1024]{1,0:T(8,128)(2,1)}, u32[]{:S(2)}) copy-start(bf16[320,1024]{1,0:T(8,128)(2,1)} %frames.7) | copy-start | bytes 1966084
  0.0 6.7 %collective-permute-start.2 = (bf16[3,1024,512]{2,1,0:T(8,128)(2,1)}, bf16[3,1024,512]{2,1,0:T(8,128)(2,1)S(1)}, u32[]{:S(2)}, u32[]{:S(2)}) collective-permute-start(bf16[3,1024,512]{2,1,0:T(8,128)(2,1)} %refs_0_.1), channel_id=1, source_target_pairs={{0,1},{1,0},{2,3},{3,2},{4,5},{5,4},{6,7},{7,6},{8,9},{9,8},{10,11... | collective-permute-start | bytes 9437192 | tf_op jit(solution)/shard_map/ppermute | solution.py:448
  0.5 10.6 %collective-permute-start.1 = (bf16[1024,512]{1,0:T(8,128)(2,1)}, bf16[1024,512]{1,0:T(8,128)(2,1)S(1)}, u32[]{:S(2)}, u32[]{:S(2)}) collective-permute-start(bf16[1024,512]{1,0:T(8,128)(2,1)} %wo.1), channel_id=1, source_target_pairs={{0,1},{1,0},{2,3},{3,2},{4,5},{5,4},{6,7},{7,6},{8,9},{9,8},{10,11... | collective-permute-start | bytes 3145736 | tf_op jit(solution)/shard_map/ppermute | solution.py:449
  0.8 3.4 %copy-start.6 = (f32[1024]{0:T(1024)S(1)}, f32[1024]{0:T(1024)}, u32[]{:S(2)}) copy-start(f32[1024]{0:T(1024)} %param.11) | copy-start | bytes 12292
  0.8 3.3 %copy-start.7 = (f32[1024]{0:T(1024)S(1)}, f32[1024]{0:T(1024)}, u32[]{:S(2)}) copy-start(f32[1024]{0:T(1024)} %param.12) | copy-start | bytes 12292
  0.9 3.3 %copy-start.8 = (s32[320]{0:T(512)S(1)}, s32[320]{0:T(512)}, u32[]{:S(2)}) copy-start(s32[320]{0:T(512)} %valid.1) | copy-start | bytes 3844
  1.1 4.1 %copy-start = (bf16[3,1024,512]{2,1,0:T(8,128)(2,1)S(1)}, bf16[3,1024,512]{2,1,0:T(8,128)(2,1)}, u32[]{:S(2)}) copy-start(bf16[3,1024,512]{2,1,0:T(8,128)(2,1)} %refs_0_.1) | copy-start | bytes 9437188
  1.2 9.9 %collective-permute-start = (bf16[1056,128]{1,0:T(8,128)(2,1)S(1)}, bf16[1056,128]{1,0:T(8,128)(2,1)S(1)}, u32[]{:S(2)}, u32[]{:S(2)}) collective-permute-start(bf16[1056,128]{1,0:T(8,128)(2,1)S(1)} %shard_map.92), channel_id=1, source_target_pairs={{1,0},{30,31},{0,2},{3,1},{2,4},{5,3},{4,6},{7,5},{6,8},{9,7},{8,1... | collective-permute-start | bytes 811016 | tf_op jit(solution)/shard_map/ppermute | solution.py:447
  11.1 2.2 %copy-start.2 = (bf16[1024,512]{1,0:T(8,128)(2,1)S(1)}, bf16[1024,512]{1,0:T(8,128)(2,1)}, u32[]{:S(2)}) copy-start(bf16[1024,512]{1,0:T(8,128)(2,1)} %wo.1) | copy-start | bytes 3145732
  11.1 2.6 %copy-start.3 = (f32[9,512]{1,0:T(8,128)S(1)}, f32[9,512]{1,0:T(8,128)}, u32[]{:S(2)}) copy-start(f32[9,512]{1,0:T(8,128)} %weight.3) | copy-start | bytes 55300
  11.1 2.6 %copy-start.4 = (f32[512]{0:T(512)S(1)}, f32[512]{0:T(512)}, u32[]{:S(2)}) copy-start(f32[512]{0:T(512)} %param.16) | copy-start | bytes 6148
  11.1 2.6 %copy-start.5 = (f32[512]{0:T(512)S(1)}, f32[512]{0:T(512)}, u32[]{:S(2)}) copy-start(f32[512]{0:T(512)} %param.17) | copy-start | bytes 6148
  13.2 1.5 %collective-permute-start.3 = (bf16[176,512]{1,0:T(8,128)(2,1)S(1)}, bf16[176,512]{1,0:T(8,128)(2,1)S(1)}, u32[]{:S(2)}, u32[]{:S(2)}) collective-permute-start(bf16[176,512]{1,0:T(8,128)(2,1)S(1)} %get-tuple-element.51), channel_id=1, source_target_pairs={{0,1},{1,0},{2,3},{3,2},{4,5},{5,4},{6,7},{7,6},{8,9},{9,8},{10,11... | collective-permute-start | bytes 540680 | tf_op jit(solution)/shard_map/ppermute | solution.py:502
